TPU v7x, 32 devices: a whole 2x2x4 slice. The times are simulated.
32 devices in a mesh: frame: 8 (over y, x, core), head: 4 (over z).
Axes of the slice: x: 2, y: 2, z: 4, core: 2. Of those that a mesh axis runs over, the one named last changes fastest.
Arguments:
- visual: bfloat16 [1024, 8192], P('frame'), may hold values from -6 to 6
- w_key: bfloat16 [8192, 1024], P(None, 'head'), may hold values from -0.0625 to 0.0625
- w_value: bfloat16 [8192, 1024], P(None, 'head'), may hold values from -0.0625 to 0.0625
- queries: float32 [256, 8192], P('frame', 'head'), may hold values from -100 to 100
- out_grad: float32 [256, 8192], P('frame', 'head'), may hold values from -6 to 6
Outputs:
- query_grad: float32 [256, 8192], P('frame', 'head')
- key_weight_grad: float32 [8192, 1024], P('frame', 'head')
- value_weight_grad: float32 [8192, 1024], P('frame', 'head')
- visual_grad: float32 [1024, 8192], P('frame', 'head')
All inputs are finite; a program needn't handle non-finite values.
Results may differ from a plain program's by a relative error of at most 0.009.
Values sent between devices are 32-bit elements; how exact they have to be, the bound alone decides.
A program may use at most 128 MiB of HBM per device.

v0:
```python
import functools

import jax
import jax.numpy as jnp
from jax import lax
from jax.experimental import pallas as pl
from jax.experimental.pallas import tpu as pltpu
from jax.sharding import PartitionSpec as P

HEAD_DIM = 128
MESH = pl.DeviceIdType.MESH
CHUNKS = 8
PIECES = 4
F32, BF16 = jnp.float32, jnp.bfloat16


def halves(a):
    high = a.astype(BF16)
    return high, (a - high.astype(F32)).astype(BF16)


def product(a, b, dims):
    (ah, al), (bh, bl) = a, b
    dot = functools.partial(
        lax.dot_general, dimension_numbers=(dims, ((), ())), preferred_element_type=F32
    )
    return dot(ah, bh) + (dot(ah, bl) + dot(al, bh))


def kernel(
    n, nh, vis, wk_any, wv_any, q, g, qg_out, kwg_out, vwg_out, vg_out,
    wk, wv, visf, visl, vist, ql, gl, kvs, kvl, parts, pre, partl, kgs, agl, qgs, qgl, vgp, zr, zl,
    w_sem, q_sems, g_sems, kv_sems, v_sems, pre_sem, part_sems, qg_sems, ag_sems, on_sems, z_sems,
):
    me, my_head = lax.axis_index("frame"), lax.axis_index("head")
    rows, depth = vis.shape
    cols = wk.shape[1]
    kv_local = cols // HEAD_DIM
    text_part, width = ql.shape[1], ql.shape[2]
    split = q.shape[0] // text_part
    heads = width // HEAD_DIM
    share = n // kv_local
    dn, dh = depth // n, depth // nh
    chunk = depth // CHUNKS
    bounds = (0, rows)
    piece = rows // PIECES
    factor = HEAD_DIM ** (-0.5)

    def frame_copy(src, dst, sems, slot_send, slot_recv, target):
        return pltpu.make_async_remote_copy(
            src_ref=src, dst_ref=dst, send_sem=sems.at[0, slot_send],
            recv_sem=sems.at[1, slot_recv], device_id={"frame": target}, device_id_type=MESH,
        )

    def frame_copy_of(src, dst, send_sem, recv_sem, target):
        return pltpu.make_async_remote_copy(
            src_ref=src, dst_ref=dst, send_sem=send_sem, recv_sem=recv_sem,
            device_id={"frame": target}, device_id_type=MESH,
        )

    def peer(k):
        return lax.rem(me + k, n)

    def source(k):
        return lax.rem(me + n - k, n)

    core, chip, chips = lax.rem(me, 2), me // 2, n // 2
    sibling = me + 1 - 2 * core

    def mate(j):
        return lax.rem(me + 2 * j, n)

    def mate_source(j):
        return lax.rem(me + n - 2 * j, n)

    def onward(land, sems, on, s):
        return frame_copy_of(land.at[s], land.at[s], on.at[s], sems.at[1, s], sibling)

    def spread(pick, land, sems):
        sends.append(frame_copy(pick(sibling), land.at[me], sems, sibling, me, sibling))
        sends[-1].start()
        for j in range(1, chips):
            p = mate(j)
            sends.append(frame_copy(pick(p), land.at[me], sems, p, me, p))
            sends[-1].start()

    def forward(land, sems, on):
        for j in range(1, chips):
            s = mate_source(j)
            frame_copy(land.at[s], land.at[s], sems, s, s, s).wait_recv()
            sends.append(onward(land, sems, on, s))
            sends[-1].start()

    def wait_rest(land, sems):
        frame_copy(land.at[sibling], land.at[sibling], sems, sibling, sibling, sibling).wait_recv()
        for j in range(1, chips):
            s = lax.rem(sibling + n - 2 * j, n)
            frame_copy(land.at[s], land.at[s], sems, s, s, sibling).wait_recv()

    loads = []
    for c in range(CHUNKS):
        at = pl.ds(c * chunk, chunk)
        for i, (src, dst) in enumerate(((wk_any, wk), (wv_any, wv))):
            loads.append(pltpu.make_async_copy(src.at[at], dst.at[at], w_sem.at[i, c]))
            loads[-1].start()

    barrier = pltpu.get_barrier_semaphore()
    for k in range(1, n):
        pl.semaphore_signal(barrier, inc=1, device_id={"frame": peer(k)}, device_id_type=MESH)
    for j in range(1, nh):
        pl.semaphore_signal(
            barrier, inc=1, device_id={"head": lax.rem(my_head + j, nh)}, device_id_type=MESH
        )
    pl.semaphore_wait(barrier, n + nh - 2)

    def text_at(p):
        part, block = lax.rem(p, split), p // split
        return (
            pl.ds(pl.multiple_of(part * text_part, text_part), text_part),
            pl.ds(pl.multiple_of(block * width, width), width),
        )

    sends = []
    for k in range(1, n):
        p = peer(k)
        for src, dst, sems in ((q, ql, q_sems), (g, gl, g_sems)):
            sends.append(frame_copy(src.at[text_at(p)], dst.at[me], sems, p, me, p))
            sends[-1].start()
    ql[me] = q[text_at(me)]
    gl[me] = g[text_at(me)]

    def stretch(i):
        return pl.ds(bounds[i], bounds[i + 1] - bounds[i])

    def send_visual(i):
        for k in range(1, n):
            p = peer(k)
            sends.append(
                frame_copy(
                    visf.at[p, stretch(i)], visl.at[me, stretch(i)], v_sems.at[i], p, me, p
                )
            )
            sends[-1].start()

    acc_k = acc_v = jnp.zeros((rows, cols), F32)
    for c in range(CHUNKS):
        loads[2 * c].wait()
        loads[2 * c + 1].wait()
        at = pl.ds(c * chunk, chunk)
        acc_k += jnp.dot(vis[:, at], wk[at], preferred_element_type=F32)
        acc_v += jnp.dot(vis[:, at], wv[at], preferred_element_type=F32)
    for a in range(kv_local):
        at = slice(a * HEAD_DIM, (a + 1) * HEAD_DIM)
        kvs[a, 0] = acc_k[:, at]
        kvs[a, 1] = acc_v[:, at]
    spread(lambda p: kvs.at[p // share], kvl, kv_sems)
    kvl[me] = kvs[me // share]


    def wait_all(land, sems):
        for k in range(1, n):
            s = source(k)
            frame_copy(land.at[s], land.at[s], sems, s, s, s).wait_recv()

    for p in range(n):
        visf[p] = vis[:, p * dn : (p + 1) * dn].astype(F32)
    forward(kvl, kv_sems, on_sems.at[0])
    wait_all(ql, q_sems)
    wait_all(gl, g_sems)
    wait_rest(kvl, kv_sems)

    keys = kvl[:, 0].reshape(n * rows, HEAD_DIM)
    values = kvl[:, 1].reshape(n * rows, HEAD_DIM)
    values2 = halves(values)
    keys_t = halves(keys.T)
    key_part = value_part = None
    for h in range(heads):
        at = slice(h * HEAD_DIM, (h + 1) * HEAD_DIM)
        query = ql[:, :, at].reshape(n * text_part, HEAD_DIM)
        grad = gl[:, :, at].reshape(n * text_part, HEAD_DIM)
        query2, grad2 = halves(query), halves(grad)
        scores = lax.dot_general(
            keys, query, (((1,), (1,)), ((), ())),
            precision=lax.Precision.HIGHEST, preferred_element_type=F32,
        ) * factor
        probs = jnp.exp(scores - jnp.max(scores, axis=0, keepdims=True))
        probs = probs * (1.0 / jnp.sum(probs, axis=0, keepdims=True))
        dprob = product(values2, grad2, ((1,), (1,)))
        delta = jnp.sum(probs * dprob, axis=0, keepdims=True)
        dscore2 = halves(probs * (dprob - delta))
        key_term = product(dscore2, query2, ((1,), (0,)))
        value_term = product(halves(probs), grad2, ((1,), (0,)))
        key_part = key_term if h == 0 else key_part + key_term
        value_part = value_term if h == 0 else value_part + value_term
        query_term = product(keys_t, dscore2, ((1,), (0,))).T * factor
        qgs[:, :, at] = query_term.reshape(n, text_part, HEAD_DIM)
    for i, part in enumerate((key_part, value_part)):
        part = part.reshape(chips, 2, rows, HEAD_DIM)
        for c in range(2):
            parts[c, :, i] = part[:, c]
    exchange = frame_copy_of(
        parts.at[1 - core], pre, pre_sem.at[0], pre_sem.at[1], sibling
    )
    exchange.start()
    exchange.wait_recv()
    sends.append(exchange)
    parts[core] += pre[...]
    for j in range(1, chips):
        p = mate(j)
        sends.append(
            frame_copy(parts.at[core, p // 2], partl.at[chip], part_sems, p // 2, chip, p)
        )
        sends[-1].start()
    partl[chip] = parts[core, chip]
    for k in range(1, n):
        p = peer(k)
        sends.append(frame_copy(qgs.at[p], qgl.at[me], qg_sems, p, me, p))
        sends[-1].start()
    qgl[me] = qgs[me]
    send_visual(0)

    for j in range(1, chips):
        s = mate_source(j)
        land = partl.at[s // 2]
        frame_copy(land, land, part_sems, s // 2, s // 2, s).wait_recv()
    low = []
    for i in range(2):
        columns = []
        for a in range(kv_local):
            total = partl[a * share // 2, i]
            for p in range(a * share // 2 + 1, (a + 1) * share // 2):
                total = total + partl[p, i]
            columns.append(total * factor if i == 0 else total)
        for a in range(kv_local):
            kgs[i, :, a * HEAD_DIM : (a + 1) * HEAD_DIM] = columns[a].astype(BF16).astype(F32)
        low.append(kgs[i].astype(BF16))

    spread(lambda p: kgs, agl, ag_sems)
    agl[me] = kgs[...]

    def visual_term(p):
        at = slice(p * dh, (p + 1) * dh)
        dims = (((1,), (1,)), ((), ()))
        vgp[p] = lax.dot_general(
            low[0], wk[at], dims, preferred_element_type=F32
        ) + lax.dot_general(low[1], wv[at], dims, preferred_element_type=F32)

    def hop(way, d, i):
        at = pl.ds(i * piece, piece)
        land = zr if way == 0 else zl
        return pltpu.make_async_remote_copy(
            src_ref=vgp.at[d, at], dst_ref=land.at[d, at], send_sem=z_sems.at[way, 0, d, i],
            recv_sem=z_sems.at[way, 1, d, i], device_id_type=MESH,
            device_id={"head": jnp.clip(my_head + 1 - 2 * way, 0, nh - 1)},
        )

    def sends_to(way, d):
        return my_head < d if way == 0 else my_head > d

    def takes_from(way):
        return my_head > 0 if way == 0 else my_head < nh - 1

    def relay(way, d, i):
        at = pl.ds(i * piece, piece)
        land = zr if way == 0 else zl

        @pl.when(sends_to(way, d))
        def _():
            @pl.when(takes_from(way))
            def _():
                hop(way, d, i).wait_recv()
                vgp[d, at] += land[d, at]

            hop(way, d, i).start()

    def columns_of(s):
        return pl.ds(pl.multiple_of(s * rows, rows), rows)

    def take_visual(k):
        s = source(k)
        for i in range(1):
            land = visl.at[s, stretch(i)]
            frame_copy(land, land, v_sems.at[i], s, s, s).wait_recv()
        vist[:, columns_of(s)] = visl[s].T.astype(BF16)

    vist[:, columns_of(me)] = visf[me].T.astype(BF16)
    far = range(nh - 1, 0, -1)
    left = list(range(1, n))
    done = set()
    for step, d in enumerate(far):
        for way, at in ((0, d), (1, nh - 1 - d)):
            if at not in done:
                visual_term(at)
                done.add(at)
        for i in range(PIECES):
            for way, at in ((0, d), (1, nh - 1 - d)):
                relay(way, at, i)
    for k in left:
        take_visual(k)

    forward(agl, ag_sems, on_sems.at[1])
    wait_rest(agl, ag_sems)
    for i, out in enumerate((kwg_out, vwg_out)):
        out[...] = jnp.dot(
            vist[...], agl[:, i].reshape(n * rows, cols).astype(BF16), preferred_element_type=F32
        )
    wait_all(qgl, qg_sems)
    for s in range(n):
        part, block = s % split, s // split
        qg_out[
            part * text_part : (part + 1) * text_part, block * width : (block + 1) * width
        ] = qgl[s]

    vg_out[...] = vgp[my_head]
    for way, land in ((0, zr), (1, zl)):

        @pl.when(takes_from(way))
        def _():
            for i in range(PIECES):
                hop(way, my_head, i).wait_recv()
            vg_out[...] += land[my_head]

        for d in range(nh):

            @pl.when(sends_to(way, d))
            def _():
                for i in range(PIECES):
                    hop(way, d, i).wait_send()

    for copy in sends:
        copy.wait_send()


def solution(mesh):
    n, nh = mesh.shape["frame"], mesh.shape["head"]

    def body(visual, w_key, w_value, queries, out_grad):
        rows, depth = visual.shape
        cols = w_key.shape[1]
        text, query_cols = queries.shape
        local_heads = query_cols // HEAD_DIM
        split = max(1, n // local_heads)
        part, width = text // split, query_cols * split // n
        vmem = pl.BlockSpec(memory_space=pltpu.VMEM)
        hbm = pl.BlockSpec(memory_space=pl.ANY)
        dn, dh = depth // n, depth // nh
        pairs = pltpu.SemaphoreType.DMA((2, n))
        return pl.pallas_call(
            functools.partial(kernel, n, nh),
            out_shape=(
                jax.ShapeDtypeStruct((text, query_cols), F32),
                jax.ShapeDtypeStruct((dn, cols), F32),
                jax.ShapeDtypeStruct((dn, cols), F32),
                jax.ShapeDtypeStruct((rows, dh), F32),
            ),
            in_specs=[vmem, hbm, hbm, vmem, vmem],
            out_specs=(vmem, vmem, vmem, vmem),
            scratch_shapes=[
                pltpu.VMEM((depth, cols), BF16),
                pltpu.VMEM((depth, cols), BF16),
                pltpu.VMEM((n, rows, dn), F32),
                pltpu.VMEM((n, rows, dn), F32),
                pltpu.VMEM((dn, n * rows), BF16),
                pltpu.VMEM((n, part, width), F32),
                pltpu.VMEM((n, part, width), F32),
                pltpu.VMEM((cols // HEAD_DIM, 2, rows, HEAD_DIM), F32),
                pltpu.VMEM((n, 2, rows, HEAD_DIM), F32),
                pltpu.VMEM((2, n // 2, 2, rows, HEAD_DIM), F32),
                pltpu.VMEM((n // 2, 2, rows, HEAD_DIM), F32),
                pltpu.VMEM((n // 2, 2, rows, HEAD_DIM), F32),
                pltpu.VMEM((2, rows, cols), F32),
                pltpu.VMEM((n, 2, rows, cols), F32),
                pltpu.VMEM((n, part, width), F32),
                pltpu.VMEM((n, part, width), F32),
                pltpu.VMEM((nh, rows, dh), F32),
                pltpu.VMEM((nh, rows, dh), F32),
                pltpu.VMEM((nh, rows, dh), F32),
                pltpu.SemaphoreType.DMA((2, CHUNKS)),
                pairs, pairs, pairs,
                pltpu.SemaphoreType.DMA((1, 2, n)),
                pltpu.SemaphoreType.DMA((2,)),
                pltpu.SemaphoreType.DMA((2, n // 2)),
                pairs, pairs, pairs,
                pltpu.SemaphoreType.DMA((2, 2, nh, PIECES)),
            ],
            compiler_params=pltpu.CompilerParams(
                collective_id=0, has_side_effects=True, vmem_limit_bytes=67000000
            ),
        )(visual, w_key, w_value, queries, out_grad)

    return jax.shard_map(
        body,
        mesh=mesh,
        in_specs=(
            P("frame", None),
            P(None, "head"),
            P(None, "head"),
            P("frame", "head"),
            P("frame", "head"),
        ),
        out_specs=(P("frame", "head"), P("frame", "head"), P("frame", "head"), P("frame", "head")),
        check_vma=False,
    )
```

profile of v0, /device:TPU:22, one launch (start us, length us, event | category | flops | bytes accessed | tf_op | source)
XLA Modules:
  0.0 131.7 jit_solution(14043826482876667856)
XLA Ops:
  0.6 123.8 %shard_map.84 = (f32[32,2048]{1,0:T(8,128)}, f32[1024,256]{1,0:T(8,128)}, f32[1024,256]{1,0:T(8,128)}, f32[128,2048]{1,0:T(8,128)}) custom-call(bf16[128,8192]{1,0:T(8,128)(2,1)} %vis.1, bf16[8192,256]{1,0:T(8,128)(2,1)} %wk_any.1, bf16[8192,256]{1,0:T(8,128)(2,1)} %wv_any.1, f32[32,2048]{1,0:T(8,128)} %q.1, f32[32,2048]{1,0:T(8,128)} %g.1), custom_call_target="tpu_custom_call" | custom-call | tf_op jit(solution)/shard_map/pallas_call | solution.py:348
  124.4 0.0 copy-start
  124.4 1.8 %copy.13 = f32[32,2048]{1,0:T(8,128)} copy(f32[32,2048]{1,0:T(8,128)} %get-tuple-element.8) | data formatting | bytes 524288
  126.2 2.3 %copy.14 = f32[1024,256]{1,0:T(8,128)} copy(f32[1024,256]{1,0:T(8,128)} %get-tuple-element.9) | data formatting | bytes 2097152
  128.5 2.3 %copy.15 = f32[1024,256]{1,0:T(8,128)} copy(f32[1024,256]{1,0:T(8,128)} %get-tuple-element.10) | data formatting | bytes 2097152
  130.7 0.0 copy-done
  130.7 1.0 copy.16
Async XLA Ops:
  124.4 6.3 %copy-start = (f32[128,2048]{1,0:T(8,128)S(1)}, f32[128,2048]{1,0:T(8,128)}, u32[]{:S(2)}) copy-start(f32[128,2048]{1,0:T(8,128)} %get-tuple-element.11) | copy-start | bytes 3145732
where the time goes:
time: 132 us
  Pallas kernels  124 us (94%)
  local copies, waits for them, and re-layouts  7.25 us (5%)
    pallas_call x1, Pallas kernels, body(): pl.pallas_call(functools.partial(kernel, n, nh), out_shape=(jax.ShapeDtyp...  124 us
    unnamed x6, local copies, waits for them, and re-layouts  7.25 us

commit v1 on v0

v1 whole, which is shorter than its diff:
```python
import functools

import jax
import jax.numpy as jnp
from jax import lax
from jax.experimental import pallas as pl
from jax.experimental.pallas import tpu as pltpu
from jax.sharding import PartitionSpec as P

HEAD_DIM = 128
MESH = pl.DeviceIdType.MESH
CHUNKS = 8
TILES = 8
UNITS = (1, 1, 2, 2, 2)
FAR, NEAR = 4, 2
LAG, MIDDLE = 3, 10
F32, BF16 = jnp.float32, jnp.bfloat16
LANES = (((1,), (1,)), ((), ()))


def halves(a):
    high = a.astype(BF16)
    return high, (a - high.astype(F32)).astype(BF16)


def product(a, b, dims):
    (ah, al), (bh, bl) = a, b
    dot = functools.partial(
        lax.dot_general, dimension_numbers=(dims, ((), ())), preferred_element_type=F32
    )
    return dot(ah, bh) + (dot(ah, bl) + dot(al, bh))


def kernel(
    n, nh, vis_any, wk_any, wv_any, q_any, g_any, qg_out, kwg_out, vwg_out, vg_out,
    vis, q, g, wk, wv, visf, visl, vist, ql, gl, kvs, kvl, parts, pre, partl, kgs, agl, kgb,
    qgs, qgl, vgp, zz, wst, wx, kgz,
    in_sems, w_sem, q_sems, g_sems, kv_sems, v_sems, pre_sems, part_sems, qg_sems, ag_sems,
    on_sems, z_sems, ws_sems, wz_sems, wx_sems, kz_sems,
):
    me, my_head = lax.axis_index("frame"), lax.axis_index("head")
    rows, depth = vis.shape
    cols = wk.shape[1]
    kv_local = cols // HEAD_DIM
    text_part, width = ql.shape[1], ql.shape[2]
    split = q.shape[0] // text_part
    heads = width // HEAD_DIM
    share = n // kv_local
    dn, dh = depth // n, depth // nh
    chunk = depth // CHUNKS
    tile = dh // TILES
    factor = HEAD_DIM ** (-0.5)
    bounds = [0]
    for u in UNITS:
        bounds.append(bounds[-1] + u * dn // sum(UNITS))
    ahead = [0] + [NEAR] * (nh - 2) + [FAR]

    def frame_copy_of(src, dst, send_sem, recv_sem, target):
        return pltpu.make_async_remote_copy(
            src_ref=src, dst_ref=dst, send_sem=send_sem, recv_sem=recv_sem,
            device_id={"frame": target}, device_id_type=MESH,
        )

    def frame_copy(src, dst, sems, slot_send, slot_recv, target):
        return frame_copy_of(src, dst, sems.at[0, slot_send], sems.at[1, slot_recv], target)

    def head_copy(src, dst, send_sem, recv_sem, target):
        return pltpu.make_async_remote_copy(
            src_ref=src, dst_ref=dst, send_sem=send_sem, recv_sem=recv_sem,
            device_id={"head": target}, device_id_type=MESH,
        )

    def peer(k):
        return lax.rem(me + k, n)

    def source(k):
        return lax.rem(me + n - k, n)

    core, chip, chips = lax.rem(me, 2), me // 2, n // 2
    sibling = me + 1 - 2 * core

    def mate(j):
        return lax.rem(me + 2 * j, n)

    def mate_source(j):
        return lax.rem(me + n - 2 * j, n)

    sends = []

    def send(copy):
        copy.start()
        sends.append(copy)

    def spread(pick, land, sems):
        send(frame_copy(pick(sibling), land.at[me], sems, sibling, me, sibling))
        for j in range(1, chips):
            p = mate(j)
            send(frame_copy(pick(p), land.at[me], sems, p, me, p))

    def forward(land, sems, on):
        for j in range(1, chips):
            s = mate_source(j)
            frame_copy(land.at[s], land.at[s], sems, s, s, s).wait_recv()
            send(frame_copy_of(land.at[s], land.at[s], on.at[s], sems.at[1, s], sibling))

    def wait_rest(land, sems):
        frame_copy(land.at[sibling], land.at[sibling], sems, sibling, sibling, sibling).wait_recv()
        for j in range(1, chips):
            s = lax.rem(sibling + n - 2 * j, n)
            frame_copy(land.at[s], land.at[s], sems, s, s, sibling).wait_recv()

    def wait_all(land, sems):
        for k in range(1, n):
            s = source(k)
            frame_copy(land.at[s], land.at[s], sems, s, s, s).wait_recv()

    def to_vmem(src, dst, sem):
        copy = pltpu.make_async_copy(src, dst, sem)
        copy.start()
        return copy

    texts_in = [to_vmem(q_any, q, in_sems.at[0]), to_vmem(g_any, g, in_sems.at[1])]
    vis_in = to_vmem(vis_any, vis, in_sems.at[2])
    loads = [
        [
            to_vmem(src.at[pl.ds(c * chunk, chunk)], dst.at[pl.ds(c * chunk, chunk)], w_sem.at[i, c])
            for c in range(CHUNKS)
        ]
        for i, (src, dst) in enumerate(((wk_any, wk), (wv_any, wv)))
    ]

    barrier = pltpu.get_barrier_semaphore()
    for k in range(1, n):
        pl.semaphore_signal(barrier, inc=1, device_id={"frame": peer(k)}, device_id_type=MESH)
    for j in range(1, nh):
        pl.semaphore_signal(
            barrier, inc=1, device_id={"head": lax.rem(my_head + j, nh)}, device_id_type=MESH
        )
    pl.semaphore_wait(barrier, n + nh - 2)

    def text_at(p):
        part, block = lax.rem(p, split), p // split
        return (
            pl.ds(pl.multiple_of(part * text_part, text_part), text_part),
            pl.ds(pl.multiple_of(block * width, width), width),
        )

    for copy, src, dst, sems in ((texts_in[0], q, ql, q_sems), (texts_in[1], g, gl, g_sems)):
        copy.wait()
        for k in range(1, n):
            p = peer(k)
            send(frame_copy(src.at[text_at(p)], dst.at[me], sems, p, me, p))
        dst[me] = src[text_at(me)]

    vis_in.wait()
    for i, w in enumerate((wk, wv)):
        acc = jnp.zeros((rows, cols), F32)
        for c in range(CHUNKS):
            loads[i][c].wait()
            at = pl.ds(c * chunk, chunk)
            acc += jnp.dot(vis[:, at], w[at], preferred_element_type=F32)
        for a in range(kv_local):
            kvs[i, a] = acc[:, a * HEAD_DIM : (a + 1) * HEAD_DIM]
        spread(lambda p, i=i: kvs.at[i, p // share], kvl.at[i], kv_sems.at[i])
        kvl[i, me] = kvs[i, me // share]

    is_end = jnp.logical_or(my_head == 0, my_head == nh - 1)
    staged = [(t, c) for t in range(nh - 1, 0, -1) for c in range(ahead[t])]
    slots = wx.shape[1]
    tw = tile // n

    def slot_of(t, c):
        return c if t == nh - 1 else jnp.where(my_head == 0, c, NEAR + c)

    def stage_copy(k):
        t, c = staged[k]
        d = jnp.where(my_head == 0, t, nh - 1 - t)
        return head_copy(
            wst.at[k], wx.at[me, slot_of(t, c)], ws_sems.at[k], wz_sems.at[slot_of(t, c)], d
        )

    if staged:

        @pl.when(is_end)
        def _():
            for k, (t, c) in enumerate(staged):
                d = jnp.where(my_head == 0, t, nh - 1 - t)
                at = pl.ds(pl.multiple_of(d * dh + c * tile + me * tw, tw), tw)
                for i, w in enumerate((wk, wv)):
                    wst[k, i] = w[at].astype(F32)
                stage_copy(k).start()

    def turn_visual(i):
        at = slice(bounds[i], bounds[i + 1])
        for p in range(n):
            block = vis[:, p * dn + bounds[i] : p * dn + bounds[i + 1]]
            visf[p, at] = block.astype(F32).T
        visl[me, at] = visf[me, at]

    def send_visual(i):
        at = pl.ds(bounds[i], bounds[i + 1] - bounds[i])
        for k in range(1, n):
            p = peer(k)
            send(frame_copy(visf.at[p, at], visl.at[me, at], v_sems.at[i], p, me, p))

    def take_visual(i):
        at = pl.ds(bounds[i], bounds[i + 1] - bounds[i])
        for k in range(1, n):
            s = source(k)
            land = visl.at[s, at]
            frame_copy(land, land, v_sems.at[i], s, s, s).wait_recv()
        for s in range(n):
            vist[at, s * rows : (s + 1) * rows] = visl[s, at].astype(BF16)
        for j, out in enumerate((kwg_out, vwg_out)):
            out[at] = jnp.dot(vist[at], kgb[j], preferred_element_type=F32)

    turn_visual(0)
    send_visual(0)
    for i in range(1, len(UNITS)):
        turn_visual(i)

    forward(kvl.at[0], kv_sems.at[0], on_sems.at[0])
    wait_all(ql, q_sems)
    wait_rest(kvl.at[0], kv_sems.at[0])
    keys = kvl[0].reshape(n * rows, HEAD_DIM)
    texts = [slice(h * HEAD_DIM, (h + 1) * HEAD_DIM) for h in range(heads)]
    queries = [ql[:, :, at].reshape(n * text_part, HEAD_DIM) for at in texts]
    probs = []
    for query in queries:
        scores = lax.dot_general(
            keys, query, LANES, precision=lax.Precision.HIGHEST, preferred_element_type=F32
        ) * factor
        raw = jnp.exp(scores - jnp.max(scores, axis=0, keepdims=True))
        probs.append(raw * (1.0 / jnp.sum(raw, axis=0, keepdims=True)))

    forward(kvl.at[1], kv_sems.at[1], on_sems.at[1])
    wait_all(gl, g_sems)
    grads2 = [halves(gl[:, :, at].reshape(n * text_part, HEAD_DIM)) for at in texts]

    def total(terms):
        out = terms[0]
        for term in terms[1:]:
            out = out + term
        return out

    def exchange(i):
        return frame_copy_of(
            parts.at[i, 1 - core], pre.at[i], pre_sems.at[i, 0], pre_sems.at[i, 1], sibling
        )

    def give(i, part):
        part = part.reshape(chips, 2, rows, HEAD_DIM)
        for c in range(2):
            parts[i, c] = part[:, c]
        send(exchange(i))

    def pass_on(i):
        exchange(i).wait_recv()
        parts[i, core] += pre[i]
        for j in range(1, chips):
            p = mate(j)
            send(
                frame_copy(
                    parts.at[i, core, p // 2], partl.at[i, chip], part_sems.at[i], p // 2, chip, p
                )
            )
        partl[i, chip] = parts[i, core, chip]

    give(1, total([product(halves(p), g2, ((1,), (0,))) for p, g2 in zip(probs, grads2)]))

    wait_rest(kvl.at[1], kv_sems.at[1])
    values2 = halves(kvl[1].reshape(n * rows, HEAD_DIM))
    dscores2 = []
    for p, g2 in zip(probs, grads2):
        dprob = product(values2, g2, ((1,), (1,)))
        delta = jnp.sum(p * dprob, axis=0, keepdims=True)
        dscores2.append(halves(p * (dprob - delta)))
    pass_on(1)
    give(0, total([product(d2, halves(query), ((1,), (0,))) for d2, query in zip(dscores2, queries)]))
    keys_t = halves(keys.T)
    for d2, at in zip(dscores2, texts):
        query_term = product(keys_t, d2, ((1,), (0,))).T * factor
        qgs[:, :, at] = query_term.reshape(n, text_part, HEAD_DIM)
    pass_on(0)
    send_visual(1)

    low = [None, None]
    for i in (1, 0):
        for j in range(1, chips):
            s = mate_source(j)
            land = partl.at[i, s // 2]
            frame_copy(land, land, part_sems.at[i], s // 2, s // 2, s).wait_recv()
        for a in range(kv_local):
            column = total([partl[i, p] for p in range(a * share // 2, (a + 1) * share // 2)])
            if i == 0:
                column = column * factor
            kgs[i, :, a * HEAD_DIM : (a + 1) * HEAD_DIM] = column.astype(BF16).astype(F32)
        low[i] = kgs[i].astype(BF16)

    lead = jnp.where(2 * my_head < nh, 0, 1)

    def block_of(way, t):
        return jnp.where(way == 0, t, nh - 1 - t)

    def rank(way):
        return jnp.where(way == 0, my_head, nh - 1 - my_head)

    def visual_term(d, c):
        at = pl.ds(pl.multiple_of(d * dh + c * tile, tile), tile)
        vgp[d, c] = lax.dot_general(
            low[0], wk[at], LANES, preferred_element_type=F32
        ) + lax.dot_general(low[1], wv[at], LANES, preferred_element_type=F32)

    def onward_head(way):
        return jnp.clip(my_head + 1 - 2 * way, 0, nh - 1)

    def hop(way, d, c):
        return head_copy(
            vgp.at[d, c], zz.at[way, d, c], z_sems.at[way, 0, d, c], z_sems.at[way, 1, d, c],
            onward_head(way),
        )

    def starts(t, c):
        return 1 if c < ahead[t] else 0

    def relay(way, t, c):
        d, first = block_of(way, t), starts(t, c)

        @pl.when(jnp.logical_and(rank(way) < t, rank(way) >= first))
        def _():
            @pl.when(rank(way) > first)
            def _():
                hop(way, d, c).wait_recv()
                vgp[d, c] += zz[way, d, c]

            hop(way, d, c).start()

    def kg_hop(way, first):
        return head_copy(
            kgs if first else kgz.at[way], kgz.at[way], kz_sems.at[way, 0], kz_sems.at[way, 1],
            onward_head(way),
        )

    def relay_grads(way):
        @pl.when(rank(way) == 0)
        def _():
            kg_hop(way, True).start()

        @pl.when(rank(way) > 0)
        def _():
            kg_hop(way, False).wait_recv()

            @pl.when(rank(way) < nh - 1)
            def _():
                kg_hop(way, False).start()

    def gather_ahead():
        for j in range(slots):
            land = wx.at[me, j]
            head_copy(land, land, wz_sems.at[j], wz_sems.at[j], my_head).wait_recv()
        spread(lambda p: wx.at[me], wx, wx_sems)

    def add_ahead():
        forward(wx, wx_sems, on_sems.at[3])
        wait_rest(wx, wx_sems)
        for j in range(slots):
            from_right = jnp.where(is_end, jnp.where(my_head == 0, 1, 0), 1 if j >= NEAR else 0)
            c = jnp.where(is_end, j, j % NEAR)
            term = vgp[my_head, c]
            for i in range(2):
                block = wx[:, j, i].reshape(tile, cols).astype(BF16)
                term += lax.dot_general(
                    kgz[from_right, i].astype(BF16), block, LANES, preferred_element_type=F32
                )
            vgp[my_head, c] = term

    spread(lambda p: kgs, agl, ag_sems)
    agl[me] = kgs[...]
    for k in range(1, n):
        p = peer(k)
        send(frame_copy(qgs.at[p], qgl.at[me], qg_sems, p, me, p))
    qgl[me] = qgs[me]
    for i in range(2, len(UNITS)):
        send_visual(i)

    def middle():
        if staged:
            gather_ahead()
        forward(agl, ag_sems, on_sems.at[2])
        wait_rest(agl, ag_sems)
        for i in range(2):
            kgb[i] = agl[:, i].reshape(n * rows, cols).astype(BF16)
        take_visual(0)
        take_visual(1)

    order = [(t, c) for t in range(nh - 1, 0, -1) for c in range(TILES)]

    def visual_terms(way, t, c):
        @pl.when(rank(way) >= starts(t, c))
        def _():
            visual_term(block_of(way, t), c)

    for k in range(len(order) + LAG):
        if k < len(order):
            t, c = order[k]
            if 2 * t > nh - 1:
                visual_terms(lead, t, c)
                visual_terms(1 - lead, t, c)
            if k == FAR:
                if staged:
                    relay_grads(lead)
            relay(lead, t, c)
        if k >= LAG:
            if k - LAG == FAR and staged:
                relay_grads(1 - lead)
            relay(1 - lead, *order[k - LAG])
        if k == MIDDLE:
            middle()

    for i in range(2, len(UNITS)):
        take_visual(i)
    wait_all(qgl, qg_sems)
    for s in range(n):
        part, block = s % split, s // split
        qg_out[
            part * text_part : (part + 1) * text_part, block * width : (block + 1) * width
        ] = qgl[s]
    if staged:
        add_ahead()

    for c in range(TILES):
        at = slice(c * tile, (c + 1) * tile)
        vg_out[:, at] = vgp[my_head, c]
        for way in (lead, 1 - lead):
            t = rank(way)
            count = jnp.where(t == nh - 1, FAR, NEAR)

            @pl.when(t > jnp.where(c < count, 1, 0))
            def _():
                hop(way, my_head, c).wait_recv()
                vg_out[:, at] += zz[way, my_head, c]

    for way in (lead, 1 - lead):
        for t, c in order:

            @pl.when(jnp.logical_and(rank(way) < t, rank(way) >= starts(t, c)))
            def _():
                hop(way, block_of(way, t), c).wait_send()

        if staged:

            @pl.when(rank(way) < nh - 1)
            def _():
                kg_hop(way, True).wait_send()

    if staged:

        @pl.when(is_end)
        def _():
            for k in range(len(staged)):
                stage_copy(k).wait_send()

    for copy in sends:
        copy.wait_send()


def store(*refs):
    outs, sems = refs[len(refs) // 2 : -1], refs[-1]
    copies = [
        pltpu.make_async_copy(src, dst, sems.at[i]) for i, (src, dst) in enumerate(zip(refs, outs))
    ]
    for copy in copies:
        copy.start()
    for copy in copies:
        copy.wait()


def solution(mesh):
    n, nh = mesh.shape["frame"], mesh.shape["head"]

    def body(visual, w_key, w_value, queries, out_grad):
        rows, depth = visual.shape
        cols = w_key.shape[1]
        text, query_cols = queries.shape
        local_heads = query_cols // HEAD_DIM
        split = max(1, n // local_heads)
        part, width = text // split, query_cols * split // n
        vmem = pl.BlockSpec(memory_space=pltpu.VMEM)
        hbm = pl.BlockSpec(memory_space=pl.ANY)
        dn, dh = depth // n, depth // nh
        tile = dh // TILES
        slots = max(FAR, 2 * NEAR, 1)
        pairs = pltpu.SemaphoreType.DMA((2, n))
        dma = pltpu.SemaphoreType.DMA
        outs = pl.pallas_call(
            functools.partial(kernel, n, nh),
            out_shape=(
                pltpu.VMEM((text, query_cols), F32),
                pltpu.VMEM((dn, cols), F32),
                pltpu.VMEM((dn, cols), F32),
                pltpu.VMEM((rows, dh), F32),
            ),
            in_specs=[hbm] * 5,
            out_specs=(vmem,) * 4,
            scratch_shapes=[
                pltpu.VMEM((rows, depth), BF16),
                pltpu.VMEM((text, query_cols), F32),
                pltpu.VMEM((text, query_cols), F32),
                pltpu.VMEM((depth, cols), BF16),
                pltpu.VMEM((depth, cols), BF16),
                pltpu.VMEM((n, dn, rows), F32),
                pltpu.VMEM((n, dn, rows), F32),
                pltpu.VMEM((dn, n * rows), BF16),
                pltpu.VMEM((n, part, width), F32),
                pltpu.VMEM((n, part, width), F32),
                pltpu.VMEM((2, cols // HEAD_DIM, rows, HEAD_DIM), F32),
                pltpu.VMEM((2, n, rows, HEAD_DIM), F32),
                pltpu.VMEM((2, 2, n // 2, rows, HEAD_DIM), F32),
                pltpu.VMEM((2, n // 2, rows, HEAD_DIM), F32),
                pltpu.VMEM((2, n // 2, rows, HEAD_DIM), F32),
                pltpu.VMEM((2, rows, cols), F32),
                pltpu.VMEM((n, 2, rows, cols), F32),
                pltpu.VMEM((2, n * rows, cols), BF16),
                pltpu.VMEM((n, part, width), F32),
                pltpu.VMEM((n, part, width), F32),
                pltpu.VMEM((nh, TILES, rows, tile), F32),
                pltpu.VMEM((2, nh, TILES, rows, tile), F32),
                pltpu.VMEM((max(FAR + NEAR * (nh - 2), 1), 2, tile // n, cols), F32),
                pltpu.VMEM((n, slots, 2, tile // n, cols), F32),
                pltpu.VMEM((2, 2, rows, cols), F32),
                dma((3,)),
                dma((2, CHUNKS)),
                pairs, pairs,
                dma((2, 2, n)),
                dma((len(UNITS), 2, n)),
                dma((2, 2)),
                dma((2, 2, n // 2)),
                pairs, pairs,
                dma((4, n)),
                dma((2, 2, nh, TILES)),
                dma((max(FAR + NEAR * (nh - 2), 1),)),
                dma((slots,)),
                pairs,
                dma((2, 2)),
            ],
            compiler_params=pltpu.CompilerParams(
                collective_id=0, has_side_effects=True, vmem_limit_bytes=60000000
            ),
        )(visual, w_key, w_value, queries, out_grad)
        return pl.pallas_call(
            store,
            out_shape=tuple(jax.ShapeDtypeStruct(o.shape, o.dtype) for o in outs),
            in_specs=[vmem] * 4,
            out_specs=(hbm,) * 4,
            scratch_shapes=[dma((4,))],
            compiler_params=pltpu.CompilerParams(vmem_limit_bytes=1 << 20),
        )(*[pltpu.with_memory_space_constraint(o, pltpu.VMEM) for o in outs])

    return jax.shard_map(
        body,
        mesh=mesh,
        in_specs=(
            P("frame", None),
            P(None, "head"),
            P(None, "head"),
            P("frame", "head"),
            P("frame", "head"),
        ),
        out_specs=(P("frame", "head"), P("frame", "head"), P("frame", "head"), P("frame", "head")),
        check_vma=False,
    )
```

time: 132 us -> 107 us (0.81)
  the two profiles are of different devices: /device:TPU:22 before, /device:TPU:0 now
where the time goes in v1:
time: 107 us
  Pallas kernels  106 us (99%)
    pallas_call x1, Pallas kernels, body(): pl.pallas_call(functools.partial(kernel, n, nh), out_shape=(pltpu.VMEM((t...  105 us

profile of v1, /device:TPU:0, one launch (start us, length us, event | category | flops | bytes accessed | tf_op | source)
XLA Modules:
  0.0 107.2 jit_solution(8868763315070284447)
XLA Ops:
  0.6 104.6 %shard_map.84 = (f32[32,2048]{1,0:T(8,128)S(1)}, f32[1024,256]{1,0:T(8,128)S(1)}, f32[1024,256]{1,0:T(8,128)S(1)}, f32[128,2048]{1,0:T(8,128)S(1)}) custom-call(bf16[128,8192]{1,0:T(8,128)(2,1)} %vis_any.1, bf16[8192,256]{1,0:T(8,128)(2,1)} %wk_any.1, bf16[8192,256]{1,0:T(8,128)(2,1)} %wv_any.1, f32[32,2048]{1,0:T(8,128)} %q_any.1, f32[32,2048]{1,0:T(8,128)} %g_any.1), custom_call_target="tpu_custom_call" | custom-call | tf_op jit(solution)/shard_map/pallas_call | solution.py:495
  105.2 1.8 %shard_map.85 = (f32[32,2048]{1,0:T(8,128)}, f32[1024,256]{1,0:T(8,128)}, f32[1024,256]{1,0:T(8,128)}, f32[128,2048]{1,0:T(8,128)}) custom-call(f32[32,2048]{1,0:T(8,128)S(1)} %get-tuple-element.8.refs_0_, f32[1024,256]{1,0:T(8,128)S(1)} %get-tuple-element.9.refs_1_, f32[1024,256]{1,0:T(8,128)S(1)} %get-tuple-element.10.refs_2_, ...), custom_call_target="tpu_custom_call" | custom-call | tf_op jit(solution)/shard_map/pallas_call | solution.py:550

commit v2 on v1

--- a/solution.py
+++ b/solution.py
@@ -11,9 +11,9 @@
 MESH = pl.DeviceIdType.MESH
 CHUNKS = 8
 TILES = 8
-UNITS = (1, 1, 2, 2, 2)
+UNITS = (2, 1, 1, 2, 2)
 FAR, NEAR = 4, 2
-LAG, MIDDLE = 3, 10
+LAG = 3
 F32, BF16 = jnp.float32, jnp.bfloat16
 LANES = (((1,), (1,)), ((), ()))
 
@@ -35,7 +35,7 @@
     n, nh, vis_any, wk_any, wv_any, q_any, g_any, qg_out, kwg_out, vwg_out, vg_out,
     vis, q, g, wk, wv, visf, visl, vist, ql, gl, kvs, kvl, parts, pre, partl, kgs, agl, kgb,
     qgs, qgl, vgp, zz, wst, wx, kgz,
-    in_sems, w_sem, q_sems, g_sems, kv_sems, v_sems, pre_sems, part_sems, qg_sems, ag_sems,
+    in_sems, w_sem, q_sems, g_sems, kv_sems, v_sems, vz_sems, pre_sems, part_sems, qg_sems, ag_sems,
     on_sems, z_sems, ws_sems, wz_sems, wx_sems, kz_sems,
 ):
     me, my_head = lax.axis_index("frame"), lax.axis_index("head")
@@ -145,24 +145,95 @@
             pl.ds(pl.multiple_of(block * width, width), width),
         )
 
-    for copy, src, dst, sems in ((texts_in[0], q, ql, q_sems), (texts_in[1], g, gl, g_sems)):
+    def send_text(copy, src, dst, sems):
         copy.wait()
         for k in range(1, n):
             p = peer(k)
             send(frame_copy(src.at[text_at(p)], dst.at[me], sems, p, me, p))
         dst[me] = src[text_at(me)]
 
-    vis_in.wait()
-    for i, w in enumerate((wk, wv)):
+    def project(i, w):
         acc = jnp.zeros((rows, cols), F32)
         for c in range(CHUNKS):
-            loads[i][c].wait()
+            if i == 0:
+                loads[i][c].wait()
             at = pl.ds(c * chunk, chunk)
             acc += jnp.dot(vis[:, at], w[at], preferred_element_type=F32)
         for a in range(kv_local):
             kvs[i, a] = acc[:, a * HEAD_DIM : (a + 1) * HEAD_DIM]
-        spread(lambda p, i=i: kvs.at[i, p // share], kvl.at[i], kv_sems.at[i])
+        spread(lambda p: kvs.at[i, p // share], kvl.at[i], kv_sems.at[i])
         kvl[i, me] = kvs[i, me // share]
+
+    quarter = bounds[1] // nh
+
+    def quarter_at(h):
+        return pl.ds(pl.multiple_of(h * quarter, quarter), quarter)
+
+    def onward_head(way):
+        return jnp.clip(my_head + 1 - 2 * way, 0, nh - 1)
+
+    def can_go(way):
+        return my_head < nh - 1 if way == 0 else my_head > 0
+
+    def quarter_copy(way, s):
+        land = visl.at[:, quarter_at(s)]
+        return head_copy(land, land, vz_sems.at[0, way, s], vz_sems.at[1, way, s], onward_head(way))
+
+    def turn_visual(i):
+        at = slice(bounds[i], bounds[i + 1])
+        for p in range(n):
+            block = vis[:, p * dn + bounds[i] : p * dn + bounds[i + 1]]
+            visf[p, at] = block.astype(F32).T
+        if i > 0:
+            visl[me, at] = visf[me, at]
+
+    def share_visual():
+        at = quarter_at(my_head)
+        visl[me, at] = visf[me, at]
+        for k in range(1, n):
+            p = peer(k)
+            send(frame_copy(visf.at[p, at], visl.at[me, at], v_sems.at[0], p, me, p))
+
+    def pass_visual():
+        at = quarter_at(my_head)
+        for k in range(1, n):
+            s = source(k)
+            frame_copy(visl.at[s, at], visl.at[s, at], v_sems.at[0], s, s, s).wait_recv()
+        for way in range(2):
+
+            @pl.when(can_go(way))
+            def _():
+                quarter_copy(way, my_head).start()
+
+    def relay_visual(j):
+        for way in range(2):
+            s = my_head - j if way == 0 else my_head + j
+
+            @pl.when(jnp.logical_and(s >= 0, s < nh))
+            def _():
+                quarter_copy(way, jnp.clip(s, 0, nh - 1)).wait_recv()
+
+                @pl.when(can_go(way))
+                def _():
+                    quarter_copy(way, jnp.clip(s, 0, nh - 1)).start()
+
+    def send_visual(i):
+        at = pl.ds(bounds[i], bounds[i + 1] - bounds[i])
+        for k in range(1, n):
+            p = peer(k)
+            send(frame_copy(visf.at[p, at], visl.at[me, at], v_sems.at[i], p, me, p))
+
+    def take_visual(i):
+        at = pl.ds(bounds[i], bounds[i + 1] - bounds[i])
+        if i > 0:
+            for k in range(1, n):
+                s = source(k)
+                land = visl.at[s, at]
+                frame_copy(land, land, v_sems.at[i], s, s, s).wait_recv()
+        for s in range(n):
+            vist[at, s * rows : (s + 1) * rows] = visl[s, at].astype(BF16)
+        for j, out in enumerate((kwg_out, vwg_out)):
+            out[at] = jnp.dot(vist[at], kgb[j], preferred_element_type=F32)
 
     is_end = jnp.logical_or(my_head == 0, my_head == nh - 1)
     staged = [(t, c) for t in range(nh - 1, 0, -1) for c in range(ahead[t])]
@@ -179,6 +250,12 @@
             wst.at[k], wx.at[me, slot_of(t, c)], ws_sems.at[k], wz_sems.at[slot_of(t, c)], d
         )
 
+    send_text(texts_in[0], q, ql, q_sems)
+    vis_in.wait()
+    turn_visual(0)
+    project(0, wk)
+    for c in range(CHUNKS):
+        loads[1][c].wait()
     if staged:
 
         @pl.when(is_end)
@@ -190,33 +267,13 @@
                     wst[k, i] = w[at].astype(F32)
                 stage_copy(k).start()
 
-    def turn_visual(i):
-        at = slice(bounds[i], bounds[i + 1])
-        for p in range(n):
-            block = vis[:, p * dn + bounds[i] : p * dn + bounds[i + 1]]
-            visf[p, at] = block.astype(F32).T
-        visl[me, at] = visf[me, at]
-
-    def send_visual(i):
-        at = pl.ds(bounds[i], bounds[i + 1] - bounds[i])
-        for k in range(1, n):
-            p = peer(k)
-            send(frame_copy(visf.at[p, at], visl.at[me, at], v_sems.at[i], p, me, p))
-
-    def take_visual(i):
-        at = pl.ds(bounds[i], bounds[i + 1] - bounds[i])
-        for k in range(1, n):
-            s = source(k)
-            land = visl.at[s, at]
-            frame_copy(land, land, v_sems.at[i], s, s, s).wait_recv()
-        for s in range(n):
-            vist[at, s * rows : (s + 1) * rows] = visl[s, at].astype(BF16)
-        for j, out in enumerate((kwg_out, vwg_out)):
-            out[at] = jnp.dot(vist[at], kgb[j], preferred_element_type=F32)
-
-    turn_visual(0)
-    send_visual(0)
-    for i in range(1, len(UNITS)):
+    send_text(texts_in[1], g, gl, g_sems)
+    share_visual()
+    project(1, wv)
+
+    turn_visual(1)
+    send_visual(1)
+    for i in range(2, len(UNITS)):
         turn_visual(i)
 
     forward(kvl.at[0], kv_sems.at[0], on_sems.at[0])
@@ -233,9 +290,16 @@
         raw = jnp.exp(scores - jnp.max(scores, axis=0, keepdims=True))
         probs.append(raw * (1.0 / jnp.sum(raw, axis=0, keepdims=True)))
 
+    pass_visual()
     forward(kvl.at[1], kv_sems.at[1], on_sems.at[1])
     wait_all(gl, g_sems)
     grads2 = [halves(gl[:, :, at].reshape(n * text_part, HEAD_DIM)) for at in texts]
+
+    def gather_ahead():
+        for j in range(slots):
+            land = wx.at[me, j]
+            head_copy(land, land, wz_sems.at[j], wz_sems.at[j], my_head).wait_recv()
+        spread(lambda p: wx.at[me], wx, wx_sems)
 
     def total(terms):
         out = terms[0]
@@ -271,18 +335,22 @@
     wait_rest(kvl.at[1], kv_sems.at[1])
     values2 = halves(kvl[1].reshape(n * rows, HEAD_DIM))
     dscores2 = []
-    for p, g2 in zip(probs, grads2):
+    for h, (p, g2) in enumerate(zip(probs, grads2)):
         dprob = product(values2, g2, ((1,), (1,)))
         delta = jnp.sum(p * dprob, axis=0, keepdims=True)
         dscores2.append(halves(p * (dprob - delta)))
-    pass_on(1)
+        if h == 0:
+            pass_on(1)
     give(0, total([product(d2, halves(query), ((1,), (0,))) for d2, query in zip(dscores2, queries)]))
     keys_t = halves(keys.T)
     for d2, at in zip(dscores2, texts):
         query_term = product(keys_t, d2, ((1,), (0,))).T * factor
         qgs[:, :, at] = query_term.reshape(n, text_part, HEAD_DIM)
     pass_on(0)
-    send_visual(1)
+    relay_visual(1)
+    if staged:
+        gather_ahead()
+    send_visual(2)
 
     low = [None, None]
     for i in (1, 0):
@@ -311,9 +379,6 @@
             low[0], wk[at], LANES, preferred_element_type=F32
         ) + lax.dot_general(low[1], wv[at], LANES, preferred_element_type=F32)
 
-    def onward_head(way):
-        return jnp.clip(my_head + 1 - 2 * way, 0, nh - 1)
-
     def hop(way, d, c):
         return head_copy(
             vgp.at[d, c], zz.at[way, d, c], z_sems.at[way, 0, d, c], z_sems.at[way, 1, d, c],
@@ -346,22 +411,18 @@
         def _():
             kg_hop(way, True).start()
 
-        @pl.when(rank(way) > 0)
+        @pl.when(jnp.logical_and(rank(way) > 0, rank(way) < nh - 1))
         def _():
             kg_hop(way, False).wait_recv()
-
-            @pl.when(rank(way) < nh - 1)
-            def _():
-                kg_hop(way, False).start()
-
-    def gather_ahead():
-        for j in range(slots):
-            land = wx.at[me, j]
-            head_copy(land, land, wz_sems.at[j], wz_sems.at[j], my_head).wait_recv()
-        spread(lambda p: wx.at[me], wx, wx_sems)
+            kg_hop(way, False).start()
 
     def add_ahead():
-        forward(wx, wx_sems, on_sems.at[3])
+        for way in range(2):
+
+            @pl.when(rank(way) == nh - 1)
+            def _():
+                kg_hop(way, False).wait_recv()
+
         wait_rest(wx, wx_sems)
         for j in range(slots):
             from_right = jnp.where(is_end, jnp.where(my_head == 0, 1, 0), 1 if j >= NEAR else 0)
@@ -380,18 +441,8 @@
         p = peer(k)
         send(frame_copy(qgs.at[p], qgl.at[me], qg_sems, p, me, p))
     qgl[me] = qgs[me]
-    for i in range(2, len(UNITS)):
+    for i in range(3, len(UNITS)):
         send_visual(i)
-
-    def middle():
-        if staged:
-            gather_ahead()
-        forward(agl, ag_sems, on_sems.at[2])
-        wait_rest(agl, ag_sems)
-        for i in range(2):
-            kgb[i] = agl[:, i].reshape(n * rows, cols).astype(BF16)
-        take_visual(0)
-        take_visual(1)
 
     order = [(t, c) for t in range(nh - 1, 0, -1) for c in range(TILES)]
 
@@ -411,13 +462,21 @@
                     relay_grads(lead)
             relay(lead, t, c)
         if k >= LAG:
-            if k - LAG == FAR and staged:
+            if k - LAG == TILES and staged:
                 relay_grads(1 - lead)
             relay(1 - lead, *order[k - LAG])
-        if k == MIDDLE:
-            middle()
-
-    for i in range(2, len(UNITS)):
+        if k == 2 and nh > 2:
+            relay_visual(2)
+
+    for j in range(3, nh):
+        relay_visual(j)
+    forward(agl, ag_sems, on_sems.at[2])
+    if staged:
+        forward(wx, wx_sems, on_sems.at[3])
+    wait_rest(agl, ag_sems)
+    for i in range(2):
+        kgb[i] = agl[:, i].reshape(n * rows, cols).astype(BF16)
+    for i in range(3):
         take_visual(i)
     wait_all(qgl, qg_sems)
     for s in range(n):
@@ -427,6 +486,8 @@
         ] = qgl[s]
     if staged:
         add_ahead()
+    for i in range(3, len(UNITS)):
+        take_visual(i)
 
     for c in range(TILES):
         at = slice(c * tile, (c + 1) * tile)
@@ -459,6 +520,14 @@
         def _():
             for k in range(len(staged)):
                 stage_copy(k).wait_send()
+
+    for way in range(2):
+        for j in range(nh):
+            s = my_head - j if way == 0 else my_head + j
+
+            @pl.when(jnp.logical_and(jnp.logical_and(s >= 0, s < nh), can_go(way)))
+            def _():
+                quarter_copy(way, jnp.clip(s, 0, nh - 1)).wait_send()
 
     for copy in sends:
         copy.wait_send()
@@ -533,6 +602,7 @@
                 pairs, pairs,
                 dma((2, 2, n)),
                 dma((len(UNITS), 2, n)),
+                dma((2, 2, nh)),
                 dma((2, 2)),
                 dma((2, 2, n // 2)),
                 pairs, pairs,

time: 107 us -> 95.1 us (0.89)
  the two profiles are of different devices: /device:TPU:0 before, /device:TPU:8 now
where the time goes in v2:
time: 95.1 us; the launch traced here: 94.5 us
  Pallas kernels  93.7 us (99%)
    pallas_call x1, Pallas kernels, body(): pl.pallas_call(functools.partial(kernel, n, nh), out_shape=(pltpu.VMEM((t...  92 us

profile of v2, /device:TPU:8, one launch (start us, length us, event | category | flops | bytes accessed | tf_op | source)
XLA Modules:
  0.0 94.5 jit_solution(8460428202394899158)
XLA Ops:
  0.6 92.0 %shard_map.84 = (f32[32,2048]{1,0:T(8,128)S(1)}, f32[1024,256]{1,0:T(8,128)S(1)}, f32[1024,256]{1,0:T(8,128)S(1)}, f32[128,2048]{1,0:T(8,128)S(1)}) custom-call(bf16[128,8192]{1,0:T(8,128)(2,1)} %vis_any.1, bf16[8192,256]{1,0:T(8,128)(2,1)} %wk_any.1, bf16[8192,256]{1,0:T(8,128)(2,1)} %wv_any.1, f32[32,2048]{1,0:T(8,128)} %q_any.1, f32[32,2048]{1,0:T(8,128)} %g_any.1), custom_call_target="tpu_custom_call" | custom-call | tf_op jit(solution)/shard_map/pallas_call | solution.py:564
  92.6 1.8 %shard_map.85 = (f32[32,2048]{1,0:T(8,128)}, f32[1024,256]{1,0:T(8,128)}, f32[1024,256]{1,0:T(8,128)}, f32[128,2048]{1,0:T(8,128)}) custom-call(f32[32,2048]{1,0:T(8,128)S(1)} %get-tuple-element.8.refs_0_, f32[1024,256]{1,0:T(8,128)S(1)} %get-tuple-element.9.refs_1_, f32[1024,256]{1,0:T(8,128)S(1)} %get-tuple-element.10.refs_2_, ...), custom_call_target="tpu_custom_call" | custom-call | tf_op jit(solution)/shard_map/pallas_call | solution.py:620

commit v3 on v2

--- a/solution.py
+++ b/solution.py
@@ -11,7 +11,7 @@
 MESH = pl.DeviceIdType.MESH
 CHUNKS = 8
 TILES = 8
-UNITS = (2, 1, 1, 2, 2)
+UNITS = (1, 1, 2, 2, 2)
 FAR, NEAR = 4, 2
 LAG = 3
 F32, BF16 = jnp.float32, jnp.bfloat16
@@ -85,11 +85,11 @@
     def mate_source(j):
         return lax.rem(me + n - 2 * j, n)
 
-    sends = []
-
-    def send(copy):
+    sends, late = [], []
+
+    def send(copy, kept=sends):
         copy.start()
-        sends.append(copy)
+        kept.append(copy)
 
     def spread(pick, land, sems):
         send(frame_copy(pick(sibling), land.at[me], sems, sibling, me, sibling))
@@ -219,9 +219,10 @@
 
     def send_visual(i):
         at = pl.ds(bounds[i], bounds[i + 1] - bounds[i])
+        kept = late if i == len(UNITS) - 1 else sends
         for k in range(1, n):
             p = peer(k)
-            send(frame_copy(visf.at[p, at], visl.at[me, at], v_sems.at[i], p, me, p))
+            send(frame_copy(visf.at[p, at], visl.at[me, at], v_sems.at[i], p, me, p), kept)
 
     def take_visual(i):
         at = pl.ds(bounds[i], bounds[i + 1] - bounds[i])
@@ -243,11 +244,16 @@
     def slot_of(t, c):
         return c if t == nh - 1 else jnp.where(my_head == 0, c, NEAR + c)
 
-    def stage_copy(k):
+    square = chips == 4
+    far_core = 6 - 2 * chip + core
+    direct = (me, far_core) if square else (me,)
+
+    def stage_copy(k, b):
         t, c = staged[k]
         d = jnp.where(my_head == 0, t, nh - 1 - t)
         return head_copy(
-            wst.at[k], wx.at[me, slot_of(t, c)], ws_sems.at[k], wz_sems.at[slot_of(t, c)], d
+            wst.at[k, b], wx.at[direct[b], slot_of(t, c)], ws_sems.at[k, b],
+            wz_sems.at[b, slot_of(t, c)], d,
         )
 
     send_text(texts_in[0], q, ql, q_sems)
@@ -262,14 +268,15 @@
         def _():
             for k, (t, c) in enumerate(staged):
                 d = jnp.where(my_head == 0, t, nh - 1 - t)
-                at = pl.ds(pl.multiple_of(d * dh + c * tile + me * tw, tw), tw)
-                for i, w in enumerate((wk, wv)):
-                    wst[k, i] = w[at].astype(F32)
-                stage_copy(k).start()
+                for b, owner in enumerate(direct):
+                    at = pl.ds(pl.multiple_of(d * dh + c * tile + owner * tw, tw), tw)
+                    for i, w in enumerate((wk, wv)):
+                        wst[k, b, i] = w[at].astype(F32)
+                    stage_copy(k, b).start()
 
     send_text(texts_in[1], g, gl, g_sems)
+    project(1, wv)
     share_visual()
-    project(1, wv)
 
     turn_visual(1)
     send_visual(1)
@@ -290,16 +297,39 @@
         raw = jnp.exp(scores - jnp.max(scores, axis=0, keepdims=True))
         probs.append(raw * (1.0 / jnp.sum(raw, axis=0, keepdims=True)))
 
-    pass_visual()
     forward(kvl.at[1], kv_sems.at[1], on_sems.at[1])
     wait_all(gl, g_sems)
     grads2 = [halves(gl[:, :, at].reshape(n * text_part, HEAD_DIM)) for at in texts]
 
     def gather_ahead():
-        for j in range(slots):
-            land = wx.at[me, j]
-            head_copy(land, land, wz_sems.at[j], wz_sems.at[j], my_head).wait_recv()
-        spread(lambda p: wx.at[me], wx, wx_sems)
+        for b, owner in enumerate(direct):
+            for j in range(slots):
+                land = wx.at[owner, j]
+                head_copy(land, land, wz_sems.at[b, j], wz_sems.at[b, j], my_head).wait_recv()
+        if square:
+            for p in near_mates(me) + [sibling]:
+                send(frame_copy(wx.at[me], wx.at[me], wx_sems, p, me, p))
+            send(frame_copy_of(wx.at[far_core], wx.at[far_core], on_sems.at[3, far_core], wx_sems.at[1, far_core], sibling))
+        else:
+            spread(lambda p: wx.at[me], wx, wx_sems)
+
+    def near_mates(d):
+        c, b = d // 2, lax.rem(d, 2)
+        return [2 * (c + 1 - 2 * lax.rem(c, 2)) + b, 2 * lax.rem(c + 2, 4) + b]
+
+    def forward_ahead():
+        if not square:
+            forward(wx, wx_sems, on_sems.at[3])
+            wait_rest(wx, wx_sems)
+            return
+        for s in near_mates(me):
+            frame_copy(wx.at[s], wx.at[s], wx_sems, s, s, s).wait_recv()
+            send(frame_copy_of(wx.at[s], wx.at[s], on_sems.at[3, s], wx_sems.at[1, s], sibling))
+
+    def rest_ahead():
+        if square:
+            for s in near_mates(sibling) + [sibling, far_core + 1 - 2 * core]:
+                frame_copy(wx.at[s], wx.at[s], wx_sems, s, s, sibling).wait_recv()
 
     def total(terms):
         out = terms[0]
@@ -342,12 +372,12 @@
         if h == 0:
             pass_on(1)
     give(0, total([product(d2, halves(query), ((1,), (0,))) for d2, query in zip(dscores2, queries)]))
+    pass_visual()
     keys_t = halves(keys.T)
     for d2, at in zip(dscores2, texts):
         query_term = product(keys_t, d2, ((1,), (0,))).T * factor
         qgs[:, :, at] = query_term.reshape(n, text_part, HEAD_DIM)
     pass_on(0)
-    relay_visual(1)
     if staged:
         gather_ahead()
     send_visual(2)
@@ -406,11 +436,12 @@
             onward_head(way),
         )
 
-    def relay_grads(way):
+    def start_grads(way):
         @pl.when(rank(way) == 0)
         def _():
             kg_hop(way, True).start()
 
+    def relay_grads(way):
         @pl.when(jnp.logical_and(rank(way) > 0, rank(way) < nh - 1))
         def _():
             kg_hop(way, False).wait_recv()
@@ -423,7 +454,7 @@
             def _():
                 kg_hop(way, False).wait_recv()
 
-        wait_rest(wx, wx_sems)
+        rest_ahead()
         for j in range(slots):
             from_right = jnp.where(is_end, jnp.where(my_head == 0, 1, 0), 1 if j >= NEAR else 0)
             c = jnp.where(is_end, j, j % NEAR)
@@ -435,14 +466,15 @@
                 )
             vgp[my_head, c] = term
 
-    spread(lambda p: kgs, agl, ag_sems)
-    agl[me] = kgs[...]
-    for k in range(1, n):
-        p = peer(k)
-        send(frame_copy(qgs.at[p], qgl.at[me], qg_sems, p, me, p))
-    qgl[me] = qgs[me]
-    for i in range(3, len(UNITS)):
-        send_visual(i)
+    def send_rows():
+        spread(lambda p: kgs, agl, ag_sems)
+        agl[me] = kgs[...]
+        for k in range(1, n):
+            p = peer(k)
+            send(frame_copy(qgs.at[p], qgl.at[me], qg_sems, p, me, p))
+        qgl[me] = qgs[me]
+        for i in range(3, len(UNITS)):
+            send_visual(i)
 
     order = [(t, c) for t in range(nh - 1, 0, -1) for c in range(TILES)]
 
@@ -451,6 +483,8 @@
         def _():
             visual_term(block_of(way, t), c)
 
+    if staged:
+        start_grads(lead)
     for k in range(len(order) + LAG):
         if k < len(order):
             t, c = order[k]
@@ -465,14 +499,26 @@
             if k - LAG == TILES and staged:
                 relay_grads(1 - lead)
             relay(1 - lead, *order[k - LAG])
-        if k == 2 and nh > 2:
+        if k == FAR - 1:
+            send_rows()
+        if k == FAR:
+            relay_visual(1)
+        if k == TILES + 2 and nh > 2:
             relay_visual(2)
+
+    def wait_hops(some):
+        for way in (lead, 1 - lead):
+            for t, c in some:
+
+                @pl.when(jnp.logical_and(rank(way) < t, rank(way) >= starts(t, c)))
+                def _():
+                    hop(way, block_of(way, t), c).wait_send()
 
     for j in range(3, nh):
         relay_visual(j)
     forward(agl, ag_sems, on_sems.at[2])
     if staged:
-        forward(wx, wx_sems, on_sems.at[3])
+        forward_ahead()
     wait_rest(agl, ag_sems)
     for i in range(2):
         kgb[i] = agl[:, i].reshape(n * rows, cols).astype(BF16)
@@ -486,8 +532,12 @@
         ] = qgl[s]
     if staged:
         add_ahead()
-    for i in range(3, len(UNITS)):
+    for i in range(3, len(UNITS) - 1):
         take_visual(i)
+    for copy in sends:
+        copy.wait_send()
+    wait_hops(order[: 2 * TILES])
+    take_visual(len(UNITS) - 1)
 
     for c in range(TILES):
         at = slice(c * tile, (c + 1) * tile)
@@ -501,13 +551,8 @@
                 hop(way, my_head, c).wait_recv()
                 vg_out[:, at] += zz[way, my_head, c]
 
+    wait_hops(order[2 * TILES :])
     for way in (lead, 1 - lead):
-        for t, c in order:
-
-            @pl.when(jnp.logical_and(rank(way) < t, rank(way) >= starts(t, c)))
-            def _():
-                hop(way, block_of(way, t), c).wait_send()
-
         if staged:
 
             @pl.when(rank(way) < nh - 1)
@@ -519,7 +564,8 @@
         @pl.when(is_end)
         def _():
             for k in range(len(staged)):
-                stage_copy(k).wait_send()
+                for b in range(len(direct)):
+                    stage_copy(k, b).wait_send()
 
     for way in range(2):
         for j in range(nh):
@@ -529,7 +575,7 @@
             def _():
                 quarter_copy(way, jnp.clip(s, 0, nh - 1)).wait_send()
 
-    for copy in sends:
+    for copy in late:
         copy.wait_send()
 
 
@@ -594,7 +640,7 @@
                 pltpu.VMEM((n, part, width), F32),
                 pltpu.VMEM((nh, TILES, rows, tile), F32),
                 pltpu.VMEM((2, nh, TILES, rows, tile), F32),
-                pltpu.VMEM((max(FAR + NEAR * (nh - 2), 1), 2, tile // n, cols), F32),
+                pltpu.VMEM((max(FAR + NEAR * (nh - 2), 1), 2, 2, tile // n, cols), F32),
                 pltpu.VMEM((n, slots, 2, tile // n, cols), F32),
                 pltpu.VMEM((2, 2, rows, cols), F32),
                 dma((3,)),
@@ -608,8 +654,8 @@
                 pairs, pairs,
                 dma((4, n)),
                 dma((2, 2, nh, TILES)),
-                dma((max(FAR + NEAR * (nh - 2), 1),)),
-                dma((slots,)),
+                dma((max(FAR + NEAR * (nh - 2), 1), 2)),
+                dma((2, slots)),
                 pairs,
                 dma((2, 2)),
             ],

time: 95.1 us -> 93.4 us (0.982)
  Pallas kernels: 93.7 us -> 92.4 us
    pallas_call x1, Pallas kernels: 92 us -> 90.7 us  [body(): pl.pallas_call(functools.partial(kernel, n, nh), out_shape=(pltpu.VMEM((t...]
where the time goes in v3:
time: 93.4 us; the launch traced here: 93.2 us
  Pallas kernels  92.4 us (99%)
    pallas_call x1, Pallas kernels, body(): pl.pallas_call(functools.partial(kernel, n, nh), out_shape=(pltpu.VMEM((t...  90.7 us

profile of v3, /device:TPU:8, one launch (start us, length us, event | category | flops | bytes accessed | tf_op | source)
XLA Modules:
  0.0 93.2 jit_solution(14228821348062562584)
XLA Ops:
  0.6 90.7 %shard_map.84 = (f32[32,2048]{1,0:T(8,128)S(1)}, f32[1024,256]{1,0:T(8,128)S(1)}, f32[1024,256]{1,0:T(8,128)S(1)}, f32[128,2048]{1,0:T(8,128)S(1)}) custom-call(bf16[128,8192]{1,0:T(8,128)(2,1)} %vis_any.1, bf16[8192,256]{1,0:T(8,128)(2,1)} %wk_any.1, bf16[8192,256]{1,0:T(8,128)(2,1)} %wv_any.1, f32[32,2048]{1,0:T(8,128)} %q_any.1, f32[32,2048]{1,0:T(8,128)} %g_any.1), custom_call_target="tpu_custom_call" | custom-call | tf_op jit(solution)/shard_map/pallas_call | solution.py:610
  91.3 1.8 %shard_map.85 = (f32[32,2048]{1,0:T(8,128)}, f32[1024,256]{1,0:T(8,128)}, f32[1024,256]{1,0:T(8,128)}, f32[128,2048]{1,0:T(8,128)}) custom-call(f32[32,2048]{1,0:T(8,128)S(1)} %get-tuple-element.8.refs_0_, f32[1024,256]{1,0:T(8,128)S(1)} %get-tuple-element.9.refs_1_, f32[1024,256]{1,0:T(8,128)S(1)} %get-tuple-element.10.refs_2_, ...), custom_call_target="tpu_custom_call" | custom-call | tf_op jit(solution)/shard_map/pallas_call | solution.py:666

commit v4 on v3

--- a/solution.py
+++ b/solution.py
@@ -13,7 +13,7 @@
 TILES = 8
 UNITS = (1, 1, 2, 2, 2)
 FAR, NEAR = 4, 2
-LAG = 3
+LAG, STORES = 3, 4
 F32, BF16 = jnp.float32, jnp.bfloat16
 LANES = (((1,), (1,)), ((), ()))
 
@@ -34,9 +34,9 @@
 def kernel(
     n, nh, vis_any, wk_any, wv_any, q_any, g_any, qg_out, kwg_out, vwg_out, vg_out,
     vis, q, g, wk, wv, visf, visl, vist, ql, gl, kvs, kvl, parts, pre, partl, kgs, agl, kgb,
-    qgs, qgl, vgp, zz, wst, wx, kgz,
+    qgs, qgl, vgp, zz, wst, wx, kgz, dsc,
     in_sems, w_sem, q_sems, g_sems, kv_sems, v_sems, vz_sems, pre_sems, part_sems, qg_sems, ag_sems,
-    on_sems, z_sems, ws_sems, wz_sems, wx_sems, kz_sems,
+    on_sems, z_sems, ws_sems, wz_sems, wx_sems, kz_sems, blk_sems,
 ):
     me, my_head = lax.axis_index("frame"), lax.axis_index("head")
     rows, depth = vis.shape
@@ -371,15 +371,47 @@
         dscores2.append(halves(p * (dprob - delta)))
         if h == 0:
             pass_on(1)
-    give(0, total([product(d2, halves(query), ((1,), (0,))) for d2, query in zip(dscores2, queries)]))
+    for h, d2 in enumerate(dscores2):
+        for i in range(2):
+            dsc[h, i] = d2[i]
+    queries2 = [halves(query) for query in queries]
+
+    def exchange_block(c):
+        return frame_copy_of(
+            parts.at[0, 1 - core, c], pre.at[0, c], blk_sems.at[0, c], blk_sems.at[1, c], sibling
+        )
+
+    def key_block(c):
+        at = pl.ds(pl.multiple_of(c * 2 * rows, 2 * rows), 2 * rows)
+        part = total(
+            [
+                product((dsc[h, 0, at], dsc[h, 1, at]), q2, ((1,), (0,)))
+                for h, q2 in enumerate(queries2)
+            ]
+        )
+        for k in range(2):
+            parts[0, k, c] = part[k * rows : (k + 1) * rows]
+        send(exchange_block(c))
+
+    def pass_block(c, p):
+        exchange_block(c).wait_recv()
+        parts[0, core, c] += pre[0, c]
+        if p is None:
+            partl[0, chip] = parts[0, core, c]
+        else:
+            send(frame_copy(parts.at[0, core, c], partl.at[0, chip], part_sems.at[0], c, chip, p))
+
+    blocks = [(mate(j) // 2, mate(j)) for j in range(1, chips)] + [(chip, None)]
+    for k, (c, p) in enumerate(blocks):
+        key_block(c)
+        if k > 0:
+            pass_block(*blocks[k - 1])
+    pass_block(*blocks[-1])
     pass_visual()
     keys_t = halves(keys.T)
     for d2, at in zip(dscores2, texts):
         query_term = product(keys_t, d2, ((1,), (0,))).T * factor
         qgs[:, :, at] = query_term.reshape(n, text_part, HEAD_DIM)
-    pass_on(0)
-    if staged:
-        gather_ahead()
     send_visual(2)
 
     low = [None, None]
@@ -473,6 +505,8 @@
             p = peer(k)
             send(frame_copy(qgs.at[p], qgl.at[me], qg_sems, p, me, p))
         qgl[me] = qgs[me]
+        if staged:
+            gather_ahead()
         for i in range(3, len(UNITS)):
             send_visual(i)
 
@@ -581,9 +615,12 @@
 
 def store(*refs):
     outs, sems = refs[len(refs) // 2 : -1], refs[-1]
-    copies = [
-        pltpu.make_async_copy(src, dst, sems.at[i]) for i, (src, dst) in enumerate(zip(refs, outs))
-    ]
+    copies = []
+    for i, (src, dst) in enumerate(zip(refs, outs)):
+        step = src.shape[0] // STORES
+        for k in range(STORES):
+            at = pl.ds(k * step, step)
+            copies.append(pltpu.make_async_copy(src.at[at], dst.at[at], sems.at[i, k]))
     for copy in copies:
         copy.start()
     for copy in copies:
@@ -643,6 +680,7 @@
                 pltpu.VMEM((max(FAR + NEAR * (nh - 2), 1), 2, 2, tile // n, cols), F32),
                 pltpu.VMEM((n, slots, 2, tile // n, cols), F32),
                 pltpu.VMEM((2, 2, rows, cols), F32),
+                pltpu.VMEM((width // HEAD_DIM, 2, n * rows, part * n), BF16),
                 dma((3,)),
                 dma((2, CHUNKS)),
                 pairs, pairs,
@@ -658,6 +696,7 @@
                 dma((2, slots)),
                 pairs,
                 dma((2, 2)),
+                dma((2, n // 2)),
             ],
             compiler_params=pltpu.CompilerParams(
                 collective_id=0, has_side_effects=True, vmem_limit_bytes=60000000
@@ -668,7 +707,7 @@
             out_shape=tuple(jax.ShapeDtypeStruct(o.shape, o.dtype) for o in outs),
             in_specs=[vmem] * 4,
             out_specs=(hbm,) * 4,
-            scratch_shapes=[dma((4,))],
+            scratch_shapes=[dma((4, STORES))],
             compiler_params=pltpu.CompilerParams(vmem_limit_bytes=1 << 20),
         )(*[pltpu.with_memory_space_constraint(o, pltpu.VMEM) for o in outs])
 

time: 93.4 us -> 92.7 us (level)
  no operation moved by 1% of the time
where the time goes in v4:
time: 92.7 us; the launch traced here: 92.6 us
  Pallas kernels  91.8 us (99%)
    pallas_call x1, Pallas kernels, body(): pl.pallas_call(functools.partial(kernel, n, nh), out_shape=(pltpu.VMEM((t...  89.9 us
    pallas_call x1, Pallas kernels, body(): pl.pallas_call(store, out_shape=tuple((jax.ShapeDtypeStruct(o.shape, o.dt...  1.88 us

profile of v4, /device:TPU:8, one launch (start us, length us, event | category | flops | bytes accessed | tf_op | source)
XLA Modules:
  0.0 92.6 jit_solution(7401914710197935237)
XLA Ops:
  0.6 89.9 %shard_map.84 = (f32[32,2048]{1,0:T(8,128)S(1)}, f32[1024,256]{1,0:T(8,128)S(1)}, f32[1024,256]{1,0:T(8,128)S(1)}, f32[128,2048]{1,0:T(8,128)S(1)}) custom-call(bf16[128,8192]{1,0:T(8,128)(2,1)} %vis_any.1, bf16[8192,256]{1,0:T(8,128)(2,1)} %wk_any.1, bf16[8192,256]{1,0:T(8,128)(2,1)} %wv_any.1, f32[32,2048]{1,0:T(8,128)} %q_any.1, f32[32,2048]{1,0:T(8,128)} %g_any.1), custom_call_target="tpu_custom_call" | custom-call | tf_op jit(solution)/shard_map/pallas_call | solution.py:647
  90.5 1.9 %shard_map.85 = (f32[32,2048]{1,0:T(8,128)}, f32[1024,256]{1,0:T(8,128)}, f32[1024,256]{1,0:T(8,128)}, f32[128,2048]{1,0:T(8,128)}) custom-call(f32[32,2048]{1,0:T(8,128)S(1)} %get-tuple-element.8.refs_0_, f32[1024,256]{1,0:T(8,128)S(1)} %get-tuple-element.9.refs_1_, f32[1024,256]{1,0:T(8,128)S(1)} %get-tuple-element.10.refs_2_, ...), custom_call_target="tpu_custom_call" | custom-call | tf_op jit(solution)/shard_map/pallas_call | solution.py:705

commit v5 on v4

--- a/solution.py
+++ b/solution.py
@@ -13,7 +13,7 @@
 TILES = 8
 UNITS = (1, 1, 2, 2, 2)
 FAR, NEAR = 4, 2
-LAG, STORES = 3, 4
+LAG, STORES = 2, 4
 F32, BF16 = jnp.float32, jnp.bfloat16
 LANES = (((1,), (1,)), ((), ()))
 
@@ -258,8 +258,8 @@
 
     send_text(texts_in[0], q, ql, q_sems)
     vis_in.wait()
-    turn_visual(0)
     project(0, wk)
+    send_text(texts_in[1], g, gl, g_sems)
     for c in range(CHUNKS):
         loads[1][c].wait()
     if staged:
@@ -274,8 +274,8 @@
                         wst[k, b, i] = w[at].astype(F32)
                     stage_copy(k, b).start()
 
-    send_text(texts_in[1], g, gl, g_sems)
     project(1, wv)
+    turn_visual(0)
     share_visual()
 
     turn_visual(1)

time: 92.7 us -> 92.6 us (level)
  no operation moved by 1% of the time
where the time goes in v5:
time: 92.6 us; the launch traced here: 92.4 us
  Pallas kernels  91.6 us (99%)
    pallas_call x1, Pallas kernels, body(): pl.pallas_call(functools.partial(kernel, n, nh), out_shape=(pltpu.VMEM((t...  89.8 us
    pallas_call x1, Pallas kernels, body(): pl.pallas_call(store, out_shape=tuple((jax.ShapeDtypeStruct(o.shape, o.dt...  1.88 us

profile of v5, /device:TPU:8, one launch (start us, length us, event | category | flops | bytes accessed | tf_op | source)
XLA Modules:
  0.0 92.4 jit_solution(4991251085300865768)
XLA Ops:
  0.6 89.8 %shard_map.84 = (f32[32,2048]{1,0:T(8,128)S(1)}, f32[1024,256]{1,0:T(8,128)S(1)}, f32[1024,256]{1,0:T(8,128)S(1)}, f32[128,2048]{1,0:T(8,128)S(1)}) custom-call(bf16[128,8192]{1,0:T(8,128)(2,1)} %vis_any.1, bf16[8192,256]{1,0:T(8,128)(2,1)} %wk_any.1, bf16[8192,256]{1,0:T(8,128)(2,1)} %wv_any.1, f32[32,2048]{1,0:T(8,128)} %q_any.1, f32[32,2048]{1,0:T(8,128)} %g_any.1), custom_call_target="tpu_custom_call" | custom-call | tf_op jit(solution)/shard_map/pallas_call | solution.py:647
  90.4 1.9 %shard_map.85 = (f32[32,2048]{1,0:T(8,128)}, f32[1024,256]{1,0:T(8,128)}, f32[1024,256]{1,0:T(8,128)}, f32[128,2048]{1,0:T(8,128)}) custom-call(f32[32,2048]{1,0:T(8,128)S(1)} %get-tuple-element.8.refs_0_, f32[1024,256]{1,0:T(8,128)S(1)} %get-tuple-element.9.refs_1_, f32[1024,256]{1,0:T(8,128)S(1)} %get-tuple-element.10.refs_2_, ...), custom_call_target="tpu_custom_call" | custom-call | tf_op jit(solution)/shard_map/pallas_call | solution.py:705
